TPU v7x, 32 devices: a whole 2x2x4 slice. The times are simulated.
32 devices in a mesh: dp: 8 (over y, x, core), tensor: 4 (over z).
Axes of the slice: x: 2, y: 2, z: 4, core: 2. Of those that a mesh axis runs over, the one named last changes fastest.
Arguments:
- hidden_in: bfloat16 [2, 8, 1024, 2048], P(None, None, ('dp', 'tensor')), may hold values from -6 to 6
- lengths: int32 [2, 8], replicated, may hold values from 1 to 1024, 6144 in all within a row
- dealing: int32 [2, 8], replicated, may hold values from 0 to 7, each once within a row
- cotangent: bfloat16 [2, 8, 1024, 2048], P(None, None, ('dp', 'tensor')), may hold values from -6 to 6
- attn_gain: bfloat16 [2048], P(('dp', 'tensor')), may hold values from 0.5 to 1.5
- attn_shift: bfloat16 [2048], P(('dp', 'tensor')), may hold values from -1.5 to 1.5
- ffn_gain: bfloat16 [2048], P(('dp', 'tensor')), may hold values from 0.5 to 1.5
- ffn_shift: bfloat16 [2048], P(('dp', 'tensor')), may hold values from -1.5 to 1.5
- qkv_weight: bfloat16 [2048, 8, 768], P('dp', 'tensor'), may hold values from -0.125 to 0.125
- qkv_bias: bfloat16 [8, 768], P('tensor', 'dp'), may hold values from -0.25 to 0.25
- dense_weight: bfloat16 [8, 256, 2048], P('tensor', 'dp'), may hold values from -1.5 to 1.5
- dense_bias: bfloat16 [2048], P(('dp', 'tensor')), may hold values from -1.5 to 1.5
- fc1_weight: bfloat16 [2048, 8192], P('dp', 'tensor'), may hold values from -0.125 to 0.125
- fc1_bias: bfloat16 [8, 1024], P('tensor', 'dp'), may hold values from -1.5 to 1.5
- fc2_weight: bfloat16 [8192, 2048], P('tensor', 'dp'), may hold values from -0.0625 to 0.0625
- fc2_bias: bfloat16 [2048], P(('dp', 'tensor')), may hold values from -1.5 to 1.5
Outputs:
- output: bfloat16 [2, 8, 1024, 2048], P(None, None, ('dp', 'tensor'))
- input_grad: bfloat16 [2, 8, 1024, 2048], P(None, None, ('dp', 'tensor'))
- attngain_grad: float32 [2048], P(('dp', 'tensor'))
- attnshift_grad: float32 [2048], P(('dp', 'tensor'))
- ffngain_grad: float32 [2048], P(('dp', 'tensor'))
- ffnshift_grad: float32 [2048], P(('dp', 'tensor'))
- qkvweight_grad: float32 [2048, 8, 768], P('dp', 'tensor')
- qkvbias_grad: float32 [8, 768], P('tensor', 'dp')
- denseweight_grad: float32 [8, 256, 2048], P('tensor', 'dp')
- densebias_grad: float32 [2048], P(('dp', 'tensor'))
- fc1weight_grad: float32 [2048, 8192], P('dp', 'tensor')
- fc1bias_grad: float32 [8, 1024], P('tensor', 'dp')
- fc2weight_grad: float32 [8192, 2048], P('tensor', 'dp')
- fc2bias_grad: float32 [2048], P(('dp', 'tensor'))
Inputs may be any that keep to these rules, and one draw needn't show every extreme that they name: lengths[m, j] belongs to the sequence in input slot dealing[m, j]; in each micro-batch the lengths sum to 6144 and the longest is 1024. Each row of dealing holds every slot number once.
All inputs are finite; a program needn't handle non-finite values.
Results may differ from a plain program's by a relative error of at most 0.013.
Values may be sent and summed in bfloat16 or wider, within the bound.
No kernel may reach another device: no remote copies, remote signals or barrier semaphores. Data moves between devices by JAX's collectives and lax.ppermute only.
A program may use at most 320 MiB of HBM per device.

v0:
```python
import math
import jax
import jax.numpy as jnp
from jax import lax
from jax.sharding import PartitionSpec as P

HD = 256
ROT = 64
EPSILON = 1e-05
ROPE_BASE = 10000.0
NEG_FILL = -1e30
SQRT_HALF = 0.7071067811865476
INV_ROOT_TWO_PI = 0.3989422804014327


def normalize(residual, gain, shift):
    centred = residual - jnp.mean(residual, axis=-1, keepdims=True)
    scaling = lax.rsqrt(jnp.mean(centred * centred, axis=-1, keepdims=True) + EPSILON)
    unit_rows = centred * scaling
    return (unit_rows * gain + shift, unit_rows, scaling)


def norm_back(grad_out, unit_rows, scaling, gain):
    grad_unit = grad_out * gain
    return scaling * (
        grad_unit
        - jnp.mean(grad_unit, axis=-1, keepdims=True)
        - unit_rows * jnp.mean(grad_unit * unit_rows, axis=-1, keepdims=True)
    )


def angles(positions):
    freqs = jnp.exp(jnp.arange(ROT // 2, dtype=jnp.float32) * (-2.0 * math.log(ROPE_BASE) / ROT))
    phases = positions.astype(jnp.float32)[:, None] * freqs[None, :]
    return (jnp.cos(phases), jnp.sin(phases))


def rotate(heads, cosines, sines):
    half_rot = ROT // 2
    lead_part = heads[..., :half_rot]
    trail_part = heads[..., half_rot:ROT]
    cos_rows = cosines[:, None, :]
    sin_rows = sines[:, None, :]
    return jnp.concatenate(
        [
            lead_part * cos_rows - trail_part * sin_rows,
            trail_part * cos_rows + lead_part * sin_rows,
            heads[..., ROT:],
        ],
        axis=-1,
    )


def take_slots(table, order):
    return jnp.take(table, order, axis=0)


def per_device(
    hidden_in,
    lengths,
    dealing,
    cotangent,
    attn_gain,
    attn_shift,
    ffn_gain,
    ffn_shift,
    qkv_weight,
    qkv_bias,
    dense_weight,
    dense_bias,
    fc1_weight,
    fc1_bias,
    fc2_weight,
    fc2_bias,
):
    n_tensor = lax.axis_size("tensor")
    n_data = lax.axis_size("dp")
    group_index = lax.axis_index("dp")
    micro_count, seq_count, piece_rows, width = hidden_in.shape
    local_rows = n_data * piece_rows
    seq_rows = n_tensor * local_rows
    block_rows = min(512, seq_rows)
    block_count = seq_rows // block_rows
    scale = 1.0 / math.sqrt(HD)
    sent_in = jax.vmap(take_slots)(hidden_in, dealing)
    sent_grad = jax.vmap(take_slots)(cotangent, dealing)
    got_in, got_grad = (
        lax.all_to_all(sent_in, "dp", split_axis=1, concat_axis=2, tiled=True),
        lax.all_to_all(sent_grad, "dp", split_axis=1, concat_axis=2, tiled=True),
    )
    small = (
        lax.all_gather(attn_gain, ("dp", "tensor"), axis=0, tiled=True),
        lax.all_gather(attn_shift, ("dp", "tensor"), axis=0, tiled=True),
        lax.all_gather(ffn_gain, ("dp", "tensor"), axis=0, tiled=True),
        lax.all_gather(ffn_shift, ("dp", "tensor"), axis=0, tiled=True),
        lax.all_gather(dense_bias, ("dp", "tensor"), axis=0, tiled=True),
        lax.all_gather(fc2_bias, ("dp", "tensor"), axis=0, tiled=True),
    )
    gain_one, shift_one, gain_two, shift_two, dense_shift, fc2_shift = [
        piece.astype(jnp.float32) for piece in small
    ]
    shard_set = (qkv_weight, qkv_bias, dense_weight, fc1_weight, fc1_bias, fc2_weight)

    def current_set():
        return (
            lax.all_gather(shard_set[0], "dp", axis=0, tiled=True),
            lax.all_gather(shard_set[1], "dp", axis=1, tiled=True),
            lax.all_gather(shard_set[2], "dp", axis=1, tiled=True),
            lax.all_gather(shard_set[3], "dp", axis=0, tiled=True),
            lax.all_gather(shard_set[4], "dp", axis=1, tiled=True),
            lax.all_gather(shard_set[5], "dp", axis=1, tiled=True),
        )

    row_ids = jnp.arange(seq_rows, dtype=jnp.int32)
    part_ids = row_ids // local_rows
    within = row_ids % local_rows
    positions = (within // piece_rows * n_tensor + part_ids) * piece_rows + within % piece_rows
    cosines, sines = angles(positions)
    my_lengths = lax.dynamic_index_in_dim(lengths, group_index, axis=1, keepdims=False)
    starts = jnp.arange(block_count, dtype=jnp.int32) * block_rows
    heads_here = qkv_weight.shape[1]
    units_here = fc1_weight.shape[1]
    weight_zero = (
        jnp.zeros((width, heads_here, 3 * HD), jnp.float32),
        jnp.zeros((heads_here, 3 * HD), jnp.float32),
        jnp.zeros((heads_here, HD, width), jnp.float32),
        jnp.zeros((width, units_here), jnp.float32),
        jnp.zeros((heads_here, units_here // heads_here), jnp.float32),
        jnp.zeros((units_here, width), jnp.float32),
    )
    small_zero = tuple((jnp.zeros((width,), jnp.float32) for index_slot in range(6)))

    def micro_step(totals, item):
        weight_totals, small_totals = totals
        rows_in, rows_grad, seq_length = item
        qkv_full, qkv_shift, dense_full, fc1_full, fc1_shift, fc2_full = current_set()
        residual = rows_in.astype(jnp.float32)
        normed_one, unit_one, scale_one = normalize(residual, gain_one, shift_one)
        normed_two = unit_one * gain_two + shift_two
        full_one, full_two = (
            lax.all_gather(normed_one.astype(jnp.bfloat16), "tensor", axis=0, tiled=True),
            lax.all_gather(normed_two.astype(jnp.bfloat16), "tensor", axis=0, tiled=True),
        )
        projected = jnp.einsum(
            "ld,dhe->lhe", full_one, qkv_full, preferred_element_type=jnp.float32
        ) + qkv_shift.astype(jnp.float32)
        queries = rotate(projected[..., :HD], cosines, sines).astype(jnp.bfloat16)
        key_rows = rotate(projected[..., HD : 2 * HD], cosines, sines).astype(jnp.bfloat16)
        value_rows = projected[..., 2 * HD :].astype(jnp.bfloat16)

        def mask_for(row_start):
            q_pos = lax.dynamic_slice_in_dim(positions, row_start, block_rows, 0)
            return (positions[None, :] <= q_pos[:, None]) & (positions[None, :] < seq_length)

        def attend(row_start):
            q_block = lax.dynamic_slice_in_dim(queries, row_start, block_rows, 0)
            scores = (
                jnp.einsum("qhe,khe->hqk", q_block, key_rows, preferred_element_type=jnp.float32)
                * scale
            )
            scores = jnp.where(mask_for(row_start)[None], scores, NEG_FILL)
            row_max = jnp.max(scores, axis=-1, keepdims=True)
            expo = jnp.exp(scores - row_max)
            row_sum = jnp.sum(expo, axis=-1, keepdims=True)
            softmax_w = (expo / row_sum).astype(jnp.bfloat16)
            mixed_block = jnp.einsum(
                "hqk,khe->qhe", softmax_w, value_rows, preferred_element_type=jnp.float32
            ).astype(jnp.bfloat16)
            return (mixed_block, (row_max + jnp.log(row_sum))[..., 0])

        mixed_blocks, lse_blocks = lax.map(attend, starts)
        mixed = mixed_blocks.reshape(seq_rows, heads_here, HD)
        attn_part = jnp.einsum("lhe,hed->ld", mixed, dense_full, preferred_element_type=jnp.float32)
        preact = jnp.dot(
            full_two, fc1_full, preferred_element_type=jnp.float32
        ) + fc1_shift.reshape(-1).astype(jnp.float32)
        activation = jax.nn.gelu(preact, approximate=False).astype(jnp.bfloat16)
        ffn_part = jnp.dot(activation, fc2_full, preferred_element_type=jnp.float32)
        branch = lax.psum_scatter(attn_part + ffn_part, "tensor", scatter_dimension=0, tiled=True)
        output_rows = (residual + branch + dense_shift + fc2_shift).astype(jnp.bfloat16)
        back_set = current_set()
        grad_full = lax.all_gather(rows_grad, "tensor", axis=0, tiled=True)
        grad_dense = jnp.einsum("lhe,ld->hed", mixed, grad_full, preferred_element_type=jnp.float32)
        grad_mixed = jnp.einsum(
            "ld,hed->lhe", grad_full, back_set[2], preferred_element_type=jnp.float32
        ).astype(jnp.bfloat16)
        grad_fc2 = jnp.einsum(
            "lf,ld->fd", activation, grad_full, preferred_element_type=jnp.float32
        )
        grad_act = jnp.einsum(
            "ld,fd->lf", grad_full, back_set[5], preferred_element_type=jnp.float32
        )
        normal_cdf = 0.5 * (1.0 + lax.erf(preact * SQRT_HALF))
        slope = normal_cdf + preact * jnp.exp(-0.5 * preact * preact) * INV_ROOT_TWO_PI
        grad_pre = (grad_act * slope).astype(jnp.bfloat16)
        grad_fc1 = jnp.einsum("ld,lf->df", full_two, grad_pre, preferred_element_type=jnp.float32)
        grad_fc1b = jnp.sum(grad_pre.astype(jnp.float32), axis=0).reshape(
            heads_here, units_here // heads_here
        )
        grad_second = jnp.einsum(
            "lf,df->ld", grad_pre, back_set[3], preferred_element_type=jnp.float32
        )

        def back_block(carry, block_item):
            key_grad, value_grad = carry
            row_start, lse_block = block_item
            q_block = lax.dynamic_slice_in_dim(queries, row_start, block_rows, 0)
            grad_block = lax.dynamic_slice_in_dim(grad_mixed, row_start, block_rows, 0)
            scores = (
                jnp.einsum("qhe,khe->hqk", q_block, key_rows, preferred_element_type=jnp.float32)
                * scale
            )
            scores = jnp.where(mask_for(row_start)[None], scores, NEG_FILL)
            softmax_f = jnp.exp(scores - lse_block[..., None])
            softmax_w = softmax_f.astype(jnp.bfloat16)
            value_grad = value_grad + jnp.einsum(
                "hqk,qhe->khe", softmax_w, grad_block, preferred_element_type=jnp.float32
            )
            grad_soft = jnp.einsum(
                "qhe,khe->hqk", grad_block, value_rows, preferred_element_type=jnp.float32
            )
            grad_scores = (
                softmax_f * (grad_soft - jnp.sum(softmax_f * grad_soft, axis=-1, keepdims=True))
            ).astype(jnp.bfloat16)
            query_part = (
                jnp.einsum(
                    "hqk,khe->qhe", grad_scores, key_rows, preferred_element_type=jnp.float32
                )
                * scale
            )
            key_grad = (
                key_grad
                + jnp.einsum(
                    "hqk,qhe->khe", grad_scores, q_block, preferred_element_type=jnp.float32
                )
                * scale
            )
            return ((key_grad, value_grad), query_part)

        zero_heads = jnp.zeros((seq_rows, heads_here, HD), jnp.float32)
        (key_grad, value_grad), query_parts = lax.scan(
            back_block, (zero_heads, zero_heads), (starts, lse_blocks)
        )
        query_grad = query_parts.reshape(seq_rows, heads_here, HD)
        grad_qkv = jnp.concatenate(
            [rotate(query_grad, cosines, -sines), rotate(key_grad, cosines, -sines), value_grad],
            axis=-1,
        ).astype(jnp.bfloat16)
        grad_qkvw = jnp.einsum(
            "ld,lhe->dhe", full_one, grad_qkv, preferred_element_type=jnp.float32
        )
        grad_qkvb = jnp.sum(grad_qkv.astype(jnp.float32), axis=0)
        grad_first = jnp.einsum(
            "lhe,dhe->ld", grad_qkv, back_set[0], preferred_element_type=jnp.float32
        )
        upstream = rows_grad.astype(jnp.float32)
        upstream_sum = jnp.sum(upstream, axis=0)
        norm_one, norm_two = (
            lax.psum_scatter(grad_first, "tensor", scatter_dimension=0, tiled=True),
            lax.psum_scatter(grad_second, "tensor", scatter_dimension=0, tiled=True),
        )
        input_rows = (
            upstream
            + norm_back(norm_one, unit_one, scale_one, gain_one)
            + norm_back(norm_two, unit_one, scale_one, gain_two)
        ).astype(jnp.bfloat16)
        small_terms = (
            jnp.sum(norm_one * unit_one, axis=0),
            jnp.sum(norm_one, axis=0),
            jnp.sum(norm_two * unit_one, axis=0),
            jnp.sum(norm_two, axis=0),
            upstream_sum,
            upstream_sum,
        )
        weight_terms = (grad_qkvw, grad_qkvb, grad_dense, grad_fc1, grad_fc1b, grad_fc2)
        new_weights = tuple((total + term for total, term in zip(weight_totals, weight_terms)))
        new_small = tuple((total + term for total, term in zip(small_totals, small_terms)))
        return ((new_weights, new_small), (output_rows, input_rows))

    (weight_totals, small_totals), (output_rows, input_rows) = lax.scan(
        micro_step, (weight_zero, small_zero), (got_in[:, 0], got_grad[:, 0], my_lengths)
    )
    weight_sums = (
        lax.psum_scatter(
            weight_totals[0].astype(jnp.bfloat16), "dp", scatter_dimension=0, tiled=True
        ).astype(jnp.float32),
        lax.psum_scatter(
            weight_totals[1].astype(jnp.bfloat16), "dp", scatter_dimension=1, tiled=True
        ).astype(jnp.float32),
        lax.psum_scatter(
            weight_totals[2].astype(jnp.bfloat16), "dp", scatter_dimension=1, tiled=True
        ).astype(jnp.float32),
        lax.psum_scatter(
            weight_totals[3].astype(jnp.bfloat16), "dp", scatter_dimension=0, tiled=True
        ).astype(jnp.float32),
        lax.psum_scatter(
            weight_totals[4].astype(jnp.bfloat16), "dp", scatter_dimension=1, tiled=True
        ).astype(jnp.float32),
        lax.psum_scatter(
            weight_totals[5].astype(jnp.bfloat16), "dp", scatter_dimension=1, tiled=True
        ).astype(jnp.float32),
    )
    small_sums = lax.psum_scatter(small_totals, ("dp", "tensor"), scatter_dimension=0, tiled=True)
    back_out, back_grad = (
        lax.all_to_all(output_rows[:, None], "dp", split_axis=2, concat_axis=1, tiled=True),
        lax.all_to_all(input_rows[:, None], "dp", split_axis=2, concat_axis=1, tiled=True),
    )
    slot_ids = jnp.arange(seq_count, dtype=jnp.int32)
    inverse = jnp.sum(
        jnp.where(dealing[:, :, None] == slot_ids[None, None, :], slot_ids[None, :, None], 0),
        axis=1,
    )
    output = jax.vmap(take_slots)(back_out, inverse)
    input_grad = jax.vmap(take_slots)(back_grad, inverse)
    return (
        output,
        input_grad,
        small_sums[0],
        small_sums[1],
        small_sums[2],
        small_sums[3],
        weight_sums[0],
        weight_sums[1],
        weight_sums[2],
        small_sums[4],
        weight_sums[3],
        weight_sums[4],
        weight_sums[5],
        small_sums[5],
    )


def solution(mesh):
    return jax.shard_map(
        per_device,
        mesh=mesh,
        in_specs=(
            P(None, None, ("dp", "tensor"), None),
            P(),
            P(),
            P(None, None, ("dp", "tensor"), None),
            P(("dp", "tensor")),
            P(("dp", "tensor")),
            P(("dp", "tensor")),
            P(("dp", "tensor")),
            P("dp", "tensor", None),
            P("tensor", "dp"),
            P("tensor", "dp", None),
            P(("dp", "tensor")),
            P("dp", "tensor"),
            P("tensor", "dp"),
            P("tensor", "dp"),
            P(("dp", "tensor")),
        ),
        out_specs=(
            P(None, None, ("dp", "tensor"), None),
            P(None, None, ("dp", "tensor"), None),
            P(("dp", "tensor")),
            P(("dp", "tensor")),
            P(("dp", "tensor")),
            P(("dp", "tensor")),
            P("dp", "tensor", None),
            P("tensor", "dp"),
            P("tensor", "dp", None),
            P(("dp", "tensor")),
            P("dp", "tensor"),
            P("tensor", "dp"),
            P("tensor", "dp"),
            P(("dp", "tensor")),
        ),
        check_vma=False,
    )
```

profile of v0, /device:TPU:0, one launch (start us, length us, event | category | flops | bytes accessed | tf_op | source)
XLA Modules:
  0.0 2300.3 jit_solution(938326112984021490)
XLA Ops:
  28.8 23.3 %all-to-all-done = bf16[2,8,32,2048]{3,2,0,1:T(8,128)(2,1)S(1)} async-done(((bf16[2,8,32,2048]{3,2,0,1:T(8,128)(2,1)}), bf16[2,8,32,2048]{3,2,0,1:T(8,128)(2,1)S(1)}, u32[]{:S(2)}, u32[]{:S(2)}) %all-to-all-start) | async-done | bytes 2097184 | tf_op jit(solution)/shard_map/all_to_all | solution.py:88
  58.2 58.6 %all-reduce.14 = (bf16[2048]{0:T(1024)(128)(2,1)S(1)}, bf16[2048]{0:T(1024)(128)(2,1)S(1)}, bf16[2048]{0:T(1024)(128)(2,1)S(1)}, bf16[2048]{0:T(1024)(128)(2,1)S...) all-reduce(bf16[2048]{0:T(1024)(128)(2,1)S(1)} %dynamic-update-slic, ...), channel_id=1, replica_groups=mesh['dp'=8,'tensor'=4] {'dp','tensor'}, use_global_device_ids=true, to_apply=%add | all-reduce | flops 12288 | bytes 49152
  127.4 1772.7 %while.89 = (s32[]{:T(128)}, f32[2048,2,768]{2,0,1:T(8,128)}, f32[2,768]{1,0:T(2,128)}, f32[2,256,2048]{2,1,0:T(8,128)}, f32[2048,2048]{1,0:T(8,128)}, /*index=5...) while((s32[]{:T(128)}, f32[2048,2,768]{2,0,1:T(8,128)}, ...), condition=%wide.region_24.26_spmd.clone.clone.clone.clone, body=%wide.region_0.25_spmd.clone.clone.clone.clone.sunk | while | flops 81338195968 | bytes 859343296 | solution.py:280
  157.5 82.4 %all-gather.26.cloned.1.call-done = bf16[1,1024,2048]{2,1,0:T(8,128)(2,1)} async-done(((bf16[1,256,2048]{2,1,0:T(8,128)(2,1)}), bf16[1,1024,2048]{2,1,0:T(8,128)(2,1)}) %all-gather.26.cloned.1.call-update) | async-done | bytes 4194320 | tf_op jit(solution)/shard_map/while/body/eval_jaxpr/all_gather | solution.py:182
  246.1 74.7 %all-gather.22.cloned.1.call-done = bf16[1024,2048]{1,0:T(8,128)(2,1)} async-done(((bf16[256,2048]{1,0:T(8,128)(2,1)}), bf16[1024,2048]{1,0:T(8,128)(2,1)}) %all-gather.22.cloned.1.call-update) | async-done | bytes 4194320 | tf_op jit(solution)/shard_map/while/body/eval_jaxpr/all_gather | solution.py:141
  320.8 47.0 %all-gather.20.cloned.1.call-done = bf16[2048,2,768]{0,2,1:T(8,128)(2,1)} async-done(((bf16[256,2,768]{0,2,1:T(8,128)(2,1)}), bf16[2048,2,768]{0,2,1:T(8,128)(2,1)}) %all-gather.20.cloned.1.call-update) | async-done | bytes 6291472 | tf_op jit(solution)/shard_map/while/body/eval_jaxpr/all_gather | solution.py:106
  386.6 17.4 while.90
  405.0 87.3 %while.91 = (s32[]{:T(128)}, f32[1024,2,256]{0,2,1:T(8,128)}, f32[1024,2,256]{0,2,1:T(8,128)}, f32[2,512,2,256]{1,0,3,2:T(2,128)}, s32[2]{0:T(128)S(1)}, /*index...) while((s32[]{:T(128)}, f32[1024,2,256]{0,2,1:T(8,128)}, ...), condition=%wide.region_9.10_spmd.clone.clone, body=%wide.region_7.9_spmd.clone.clone.sunk | while | flops 2704015360 | bytes 111194568 | solution.py:241
  421.3 19.6 dynamic_update_slice.44
  463.7 19.6 dynamic_update_slice.44
  538.0 31.3 %fusion.250 = (bf16[1024,2048]{1,0:T(8,128)(2,1)}, f32[1024,2048]{1,0:T(8,128)}) fusion(f32[2048]{0:T(1024)S(1)} %bitcast.334, bf16[1024,2048]{1,0:T(8,128)(2,1)} %all-gather.28.cloned.1.call-done, bf16[2048,2048]{1,0:T(8,128)(2,1)} %all-gather.30.cloned.1.call-done), kind=kOutput, calls=%fused_computation.67.clone.1 | convolution fusion | flops 8728346624 | bytes 25174016 | tf_op jit(solution)/shard_map/while/body/eval_jaxpr/dot_general | solution.py:174
  665.1 44.9 %reduce-scatter.25.cloned.1.call-done = f32[256,2048]{1,0:T(8,128)} async-done(((f32[1024,2048]{1,0:T(8,128)}), f32[256,2048]{1,0:T(8,128)}) %reduce-scatter.25.cloned.1.call-update) | async-done | bytes 2097168 | tf_op jit(solution)/shard_map/while/body/eval_jaxpr/reduce_scatter | solution.py:259
  710.0 147.6 %reduce-scatter.23.cloned.1.call-done = f32[256,2048]{1,0:T(8,128)} async-done(((f32[1024,2048]{1,0:T(8,128)}), f32[256,2048]{1,0:T(8,128)}) %reduce-scatter.23.cloned.1.call-update) | async-done | bytes 2097168 | tf_op jit(solution)/shard_map/while/body/eval_jaxpr/reduce_scatter | solution.py:260
  861.8 143.2 %reduce-scatter.27.cloned.1.call-done = f32[256,2048]{1,0:T(8,128)} async-done(((f32[1024,2048]{1,0:T(8,128)}), f32[256,2048]{1,0:T(8,128)}) %reduce-scatter.27.cloned.1.call-update) | async-done | bytes 2097168 | tf_op jit(solution)/shard_map/while/body/eval_jaxpr/reduce_scatter | solution.py:179
  1041.8 82.2 %all-gather.26.cloned.1.call-done = bf16[1,1024,2048]{2,1,0:T(8,128)(2,1)} async-done(((bf16[1,256,2048]{2,1,0:T(8,128)(2,1)}), bf16[1,1024,2048]{2,1,0:T(8,128)(2,1)}) %all-gather.26.cloned.1.call-update) | async-done | bytes 4194320 | tf_op jit(solution)/shard_map/while/body/eval_jaxpr/all_gather | solution.py:182
  1130.2 74.7 %all-gather.22.cloned.1.call-done = bf16[1024,2048]{1,0:T(8,128)(2,1)} async-done(((bf16[256,2048]{1,0:T(8,128)(2,1)}), bf16[1024,2048]{1,0:T(8,128)(2,1)}) %all-gather.22.cloned.1.call-update) | async-done | bytes 4194320 | tf_op jit(solution)/shard_map/while/body/eval_jaxpr/all_gather | solution.py:141
  1204.9 47.0 %all-gather.20.cloned.1.call-done = bf16[2048,2,768]{0,2,1:T(8,128)(2,1)} async-done(((bf16[256,2,768]{0,2,1:T(8,128)(2,1)}), bf16[2048,2,768]{0,2,1:T(8,128)(2,1)}) %all-gather.20.cloned.1.call-update) | async-done | bytes 6291472 | tf_op jit(solution)/shard_map/while/body/eval_jaxpr/all_gather | solution.py:106
  1270.8 17.4 while.90
  1289.2 87.3 %while.91 = (s32[]{:T(128)}, f32[1024,2,256]{0,2,1:T(8,128)}, f32[1024,2,256]{0,2,1:T(8,128)}, f32[2,512,2,256]{1,0,3,2:T(2,128)}, s32[2]{0:T(128)S(1)}, /*index...) while((s32[]{:T(128)}, f32[1024,2,256]{0,2,1:T(8,128)}, ...), condition=%wide.region_9.10_spmd.clone.clone, body=%wide.region_7.9_spmd.clone.clone.sunk | while | flops 2704015360 | bytes 111194568 | solution.py:241
  1305.5 19.6 dynamic_update_slice.44
  1347.9 19.6 dynamic_update_slice.44
  1422.2 31.4 %fusion.250 = (bf16[1024,2048]{1,0:T(8,128)(2,1)}, f32[1024,2048]{1,0:T(8,128)}) fusion(f32[2048]{0:T(1024)S(1)} %bitcast.334, bf16[1024,2048]{1,0:T(8,128)(2,1)} %all-gather.28.cloned.1.call-done, bf16[2048,2048]{1,0:T(8,128)(2,1)} %all-gather.30.cloned.1.call-done), kind=kOutput, calls=%fused_computation.67.clone.1 | convolution fusion | flops 8728346624 | bytes 25174016 | tf_op jit(solution)/shard_map/while/body/eval_jaxpr/dot_general | solution.py:174
  1524.7 18.5 select_add_fusion.24
  1559.4 34.4 %reduce-scatter.25.cloned.1.call-done = f32[256,2048]{1,0:T(8,128)} async-done(((f32[1024,2048]{1,0:T(8,128)}), f32[256,2048]{1,0:T(8,128)}) %reduce-scatter.25.cloned.1.call-update) | async-done | bytes 2097168 | tf_op jit(solution)/shard_map/while/body/eval_jaxpr/reduce_scatter | solution.py:259
  1593.8 147.6 %reduce-scatter.23.cloned.1.call-done = f32[256,2048]{1,0:T(8,128)} async-done(((f32[1024,2048]{1,0:T(8,128)}), f32[256,2048]{1,0:T(8,128)}) %reduce-scatter.23.cloned.1.call-update) | async-done | bytes 2097168 | tf_op jit(solution)/shard_map/while/body/eval_jaxpr/reduce_scatter | solution.py:260
  1745.6 143.2 %reduce-scatter.27.cloned.1.call-done = f32[256,2048]{1,0:T(8,128)} async-done(((f32[1024,2048]{1,0:T(8,128)}), f32[256,2048]{1,0:T(8,128)}) %reduce-scatter.27.cloned.1.call-update) | async-done | bytes 2097168 | tf_op jit(solution)/shard_map/while/body/eval_jaxpr/reduce_scatter | solution.py:179
  1907.4 21.9 copy.230
  1961.7 22.5 all-to-all-done.3
  1990.1 64.1 %all-reduce.13 = (f32[2048]{0:T(1024)S(1)}, f32[2048]{0:T(1024)S(1)}, f32[2048]{0:T(1024)S(1)}, f32[2048]{0:T(1024)S(1)}, f32[2048]{0:T(1024)S(1)}, /*index=5*/f32[2048]{0:T(1024)S(1)}) all-reduce(f32[2048]{0:T(1024)S(1)} %copy-done.33, f32[2048]{0:T(1024)S(1)} %copy-done.36, ...), channel_id=6, replica_groups=mesh['dp'=8,'tensor'=4] {'dp','tensor'}, use_global_device_ids=true, to_apply=%region_26.28.clone | all-reduce | flops 12288 | bytes 98304
  2077.5 62.7 %all-reduce.17.cloned.1.call-done = bf16[2048,2,768]{2,1,0:T(2,128)(2,1)} async-done(((bf16[2048,2,768]{2,1,0:T(2,128)(2,1)}), bf16[2048,2,768]{2,1,0:T(2,128)(2,1)}) %all-reduce.17.cloned.1.call-update) | async-done | bytes 6291472
  2143.0 72.0 %reduce-scatter.15.cloned.1.call-done = bf16[256,2048]{1,0:T(8,128)(2,1)} async-done(((bf16[2048,2048]{1,0:T(8,128)(2,1)}), bf16[256,2048]{1,0:T(8,128)(2,1)}) %reduce-scatter.15.cloned.1.call-update) | async-done | bytes 1048592 | tf_op jit(solution)/shard_map/reduce_scatter | solution.py:293
  2217.7 72.2 %reduce-scatter.17.cloned.1.call-done = bf16[2048,256]{1,0:T(8,128)(2,1)} async-done(((bf16[2048,2048]{1,0:T(8,128)(2,1)}), bf16[2048,256]{1,0:T(8,128)(2,1)}) %reduce-scatter.17.cloned.1.call-update) | async-done | bytes 1048592 | tf_op jit(solution)/shard_map/reduce_scatter | solution.py:299
  (635 shorter events, 632.4 us)
Async XLA Ops:
  20.3 31.8 %all-to-all-start = ((bf16[2,8,32,2048]{3,2,0,1:T(8,128)(2,1)}), bf16[2,8,32,2048]{3,2,0,1:T(8,128)(2,1)S(1)}, u32[]{:S(2)}, u32[]{:S(2)}) async-start(bf16[2,8,32,2048]{3,2,0,1:T(8,128)(2,1)} %copy.186), calls=%async_computation.3 | async-start | bytes 4194304 | tf_op jit(solution)/shard_map/all_to_all | solution.py:88
  52.1 72.2 %all-to-all-start.1 = ((bf16[2,8,32,2048]{3,2,0,1:T(8,128)(2,1)}), bf16[2,8,32,2048]{3,2,0,1:T(8,128)(2,1)}, u32[]{:S(2)}, u32[]{:S(2)}) async-start(bf16[2,8,32,2048]{3,2,0,1:T(8,128)(2,1)} %copy.188), calls=%async_computation.4 | async-start | bytes 4194304 | tf_op jit(solution)/shard_map/all_to_all | solution.py:89
  127.8 29.7 %all-gather.24.cloned.1.call-start = ((), (), s32[]{:S(2)}) async-start(), calls=%async_computation.20 | async-start | bytes 2359296 | tf_op jit(solution)/shard_map/while/body/eval_jaxpr/all_gather | solution.py:108
  128.5 111.3 %all-gather.26.cloned.1.call-start = ((), (), s32[]{:S(2)}) async-start(), calls=%async_computation.21 | async-start | bytes 5242880 | tf_op jit(solution)/shard_map/while/body/eval_jaxpr/all_gather | solution.py:182
  131.7 189.1 %all-gather.22.cloned.1.call-start = ((), (), s32[]{:S(2)}) async-start(), calls=%async_computation.19 | async-start | bytes 5242880 | tf_op jit(solution)/shard_map/while/body/eval_jaxpr/all_gather | solution.py:141
  135.4 232.4 %all-gather.20.cloned.1.call-start = ((), (), s32[]{:S(2)}) async-start(), calls=%async_computation.18 | async-start | bytes 7077888 | tf_op jit(solution)/shard_map/while/body/eval_jaxpr/all_gather | solution.py:106
  135.9 402.0 %all-gather.28.cloned.1.call-start = ((), (), s32[]{:S(2)}) async-start(), calls=%async_computation.22 | async-start | bytes 5242880 | tf_op jit(solution)/shard_map/while/body/eval_jaxpr/all_gather | solution.py:142
  136.5 401.5 %all-gather.30.cloned.1.call-start = ((), (), s32[]{:S(2)}) async-start(), calls=%async_computation.23 | async-start | bytes 9437184 | tf_op jit(solution)/shard_map/while/body/eval_jaxpr/all_gather | solution.py:109
  137.1 432.2 %all-gather.32.cloned.1.call-start = ((), (), s32[]{:S(2)}) async-start(), calls=%async_computation.24 | async-start | bytes 9437184 | tf_op jit(solution)/shard_map/while/body/eval_jaxpr/all_gather | solution.py:111
  137.9 572.1 %reduce-scatter.25.cloned.1.call-start = ((), (), s32[]{:S(2)}) async-start(), calls=%async_computation.26 | async-start | bytes 10485760 | tf_op jit(solution)/shard_map/while/body/eval_jaxpr/reduce_scatter | solution.py:259
  528.6 329.0 %reduce-scatter.23.cloned.1.call-start = ((), (), s32[]{:S(2)}) async-start(), calls=%async_computation.25 | async-start | bytes 10485760 | tf_op jit(solution)/shard_map/while/body/eval_jaxpr/reduce_scatter | solution.py:260
  599.9 405.1 %reduce-scatter.27.cloned.1.call-start = ((), (), s32[]{:S(2)}) async-start(), calls=%async_computation.27 | async-start | bytes 10485760 | tf_op jit(solution)/shard_map/while/body/eval_jaxpr/reduce_scatter | solution.py:179
  665.0 340.0 %copy-start.13 = (bf16[1,256,2048]{2,1,0:T(8,128)(2,1)S(1)}, bf16[1,256,2048]{2,1,0:T(8,128)(2,1)}, u32[]{:S(2)}) copy-start(bf16[1,256,2048]{2,1,0:T(8,128)(2,1)} %get-tuple-element.1932) | copy-start | bytes 3145732 | tf_op jit(solution)/shard_map/while
  665.0 340.0 %copy-start.49 = (f32[2048]{0:T(1024)S(1)}, f32[2048]{0:T(1024)}, u32[]{:S(2)}) copy-start(f32[2048]{0:T(1024)} %get-tuple-element.2181) | copy-start | bytes 24580 | tf_op jit(solution)/shard_map/while
  1010.4 31.4 %all-gather.24.cloned.1.call-start = ((), (), s32[]{:S(2)}) async-start(), calls=%async_computation.20 | async-start | bytes 2359296 | tf_op jit(solution)/shard_map/while/body/eval_jaxpr/all_gather | solution.py:108
  1011.1 112.9 %all-gather.26.cloned.1.call-start = ((), (), s32[]{:S(2)}) async-start(), calls=%async_computation.21 | async-start | bytes 5242880 | tf_op jit(solution)/shard_map/while/body/eval_jaxpr/all_gather | solution.py:182
  1014.3 190.6 %all-gather.22.cloned.1.call-start = ((), (), s32[]{:S(2)}) async-start(), calls=%async_computation.19 | async-start | bytes 5242880 | tf_op jit(solution)/shard_map/while/body/eval_jaxpr/all_gather | solution.py:141
  1018.0 233.9 %all-gather.20.cloned.1.call-start = ((), (), s32[]{:S(2)}) async-start(), calls=%async_computation.18 | async-start | bytes 7077888 | tf_op jit(solution)/shard_map/while/body/eval_jaxpr/all_gather | solution.py:106
  1018.5 403.6 %all-gather.28.cloned.1.call-start = ((), (), s32[]{:S(2)}) async-start(), calls=%async_computation.22 | async-start | bytes 5242880 | tf_op jit(solution)/shard_map/while/body/eval_jaxpr/all_gather | solution.py:142
  1019.1 403.0 %all-gather.30.cloned.1.call-start = ((), (), s32[]{:S(2)}) async-start(), calls=%async_computation.23 | async-start | bytes 9437184 | tf_op jit(solution)/shard_map/while/body/eval_jaxpr/all_gather | solution.py:109
  1019.7 433.8 %all-gather.32.cloned.1.call-start = ((), (), s32[]{:S(2)}) async-start(), calls=%async_computation.24 | async-start | bytes 9437184 | tf_op jit(solution)/shard_map/while/body/eval_jaxpr/all_gather | solution.py:111
  1020.3 573.5 %reduce-scatter.25.cloned.1.call-start = ((), (), s32[]{:S(2)}) async-start(), calls=%async_computation.26 | async-start | bytes 10485760 | tf_op jit(solution)/shard_map/while/body/eval_jaxpr/reduce_scatter | solution.py:259
  1412.7 328.7 %reduce-scatter.23.cloned.1.call-start = ((), (), s32[]{:S(2)}) async-start(), calls=%async_computation.25 | async-start | bytes 10485760 | tf_op jit(solution)/shard_map/while/body/eval_jaxpr/reduce_scatter | solution.py:260
  1484.0 404.8 %reduce-scatter.27.cloned.1.call-start = ((), (), s32[]{:S(2)}) async-start(), calls=%async_computation.27 | async-start | bytes 10485760 | tf_op jit(solution)/shard_map/while/body/eval_jaxpr/reduce_scatter | solution.py:179
  1900.2 157.4 %reduce-scatter.19.cloned.1.call-start = ((), (), s32[]{:S(2)}) async-start(), calls=%async_computation.15 | async-start | bytes 221184
  1901.8 157.2 %reduce-scatter.21.cloned.1.call-start = ((), (), s32[]{:S(2)}) async-start(), calls=%async_computation.16 | async-start | bytes 294912
  1903.5 172.0 %reduce-scatter.13.cloned.1.call-start = ((), (), s32[]{:S(2)}) async-start(), calls=%async_computation.12 | async-start | bytes 2359296 | tf_op jit(solution)/shard_map/reduce_scatter | solution.py:290
  1907.4 232.8 %all-reduce.17.cloned.1.call-start = ((), (), s32[]{:S(2)}) async-start(), calls=%async_computation.17 | async-start | bytes 12582912
  1929.4 285.5 %reduce-scatter.15.cloned.1.call-start = ((), (), s32[]{:S(2)}) async-start(), calls=%async_computation.13 | async-start | bytes 9437184 | tf_op jit(solution)/shard_map/reduce_scatter | solution.py:293
  1938.6 351.4 %reduce-scatter.17.cloned.1.call-start = ((), (), s32[]{:S(2)}) async-start(), calls=%async_computation.14 | async-start | bytes 9437184 | tf_op jit(solution)/shard_map/reduce_scatter | solution.py:299
  1952.8 31.4 %all-to-all-start.3 = ((bf16[2,1,256,2048]{3,0,1,2:T(2,128)(2,1)}), bf16[2,1,256,2048]{3,0,1,2:T(2,128)(2,1)S(1)}, u32[]{:S(2)}, u32[]{:S(2)}) async-start(bf16[2,1,256,2048]{3,0,1,2:T(2,128)(2,1)} %bitcast.325), calls=%async_computation.6 | async-start | bytes 4194304 | tf_op jit(solution)/shard_map/all_to_all | solution.py:306
  1984.2 82.0 %all-to-all-start.2 = ((bf16[2,1,256,2048]{3,0,1,2:T(2,128)(2,1)}), bf16[2,1,256,2048]{3,0,1,2:T(2,128)(2,1)}, u32[]{:S(2)}, u32[]{:S(2)}) async-start(bf16[2,1,256,2048]{3,0,1,2:T(2,128)(2,1)} %bitcast.324), calls=%async_computation.5 | async-start | bytes 4194304 | tf_op jit(solution)/shard_map/all_to_all | solution.py:305
  (138 other events, 6812.9 us)
Sparse Core Ops, SparseCore 0:
  130.6 26.9 all-gather.23
  159.1 80.7 all-gather.25
  241.5 79.2 all-gather.21
  322.5 45.1 all-gather.19
  369.7 80.7 all-gather.27
  452.3 52.9 all-gather.29
  507.1 55.9 all-gather.31
  565.5 144.4 reduce-scatter.24
  712.3 145.1 reduce-scatter.22
  859.8 145.1 reduce-scatter.26
  1013.1 28.6 all-gather.23
  1043.2 80.7 all-gather.25
  1125.6 79.2 all-gather.21
  1206.7 45.1 all-gather.19
  1253.9 80.7 all-gather.27
  1336.4 52.9 all-gather.29
  1391.1 55.9 all-gather.31
  1449.3 144.4 reduce-scatter.24
  1596.2 145.1 reduce-scatter.22
  1743.6 145.1 reduce-scatter.26
Sparse Core Ops, SparseCore 1:
  1904.2 34.2 reduce-scatter.18
  1942.3 34.7 reduce-scatter.20
  1980.2 51.9 reduce-scatter.12
  2035.8 104.3 all-reduce.16
  2143.6 71.2 reduce-scatter.14
  2218.8 71.1 reduce-scatter.16
where the time goes:
time: 2310 us; the launch traced here: 2300 us
  waiting for transfers between devices  1340 us (58%)
  matrix products  387 us (17%)
  local copies, waits for them, and re-layouts  238 us (10%)
  blocking collectives  159 us (7%)
  other arithmetic  111 us (5%)
  loops' own time  25.3 us (1%)
    reduce_scatter x2, waiting for transfers between devices, micro_step(): lax.psum_scatter(grad_second, 'tensor', scatter_dimension=0, tiled=True)  295 us
    reduce_scatter x2, waiting for transfers between devices, micro_step(): lax.psum_scatter(attn_part + ffn_part, 'tensor', scatter_dimension=0, til...  286 us
    all_gather x2, waiting for transfers between devices, micro_step(): grad_full = lax.all_gather(rows_grad, 'tensor', axis=0, tiled=True)  165 us
    all_gather x2, waiting for transfers between devices, micro_step(): lax.all_gather(normed_one.astype(jnp.bfloat16), 'tensor', axis=0, tiled=T...  149 us
    unnamed x2, blocking collectives  123 us
    all_gather x2, waiting for transfers between devices, current_set(): lax.all_gather(shard_set[0], 'dp', axis=0, tiled=True)  93.9 us
    dynamic_update_slice x8, local copies, waits for them, and re-layouts, micro_step(): lax.scan(back_block, (zero_heads, zero_heads), (starts, lse_blocks))  92.7 us
    reduce_scatter x2, waiting for transfers between devices, micro_step(): lax.psum_scatter(grad_first, 'tensor', scatter_dimension=0, tiled=True)  79.3 us
  transfers between devices with their start and end apart: 30, of which 19 were waited for; matrix products, arithmetic and copies ran while one was open for 30% of the time, Pallas kernels for 0%

commit v1 on v0

--- a/solution.py
+++ b/solution.py
@@ -11,6 +11,24 @@
 NEG_FILL = -1e30
 SQRT_HALF = 0.7071067811865476
 INV_ROOT_TWO_PI = 0.3989422804014327
+
+
+def gather_around(shard, axis, dim):
+    ways, here, step = (lax.axis_size(axis), lax.axis_index(axis), shard.shape[dim])
+    shape = [n * ways if d == dim else n for d, n in enumerate(shard.shape)]
+    full = lax.dynamic_update_slice_in_dim(
+        jnp.zeros(shape, shard.dtype), shard, here * step, axis=dim
+    )
+    going_up = going_down = shard
+    for far in range(1, ways // 2 + 1):
+        going_up = lax.ppermute(going_up, axis, [(d, (d + 1) % ways) for d in range(ways)])
+        full = lax.dynamic_update_slice_in_dim(full, going_up, (here - far) % ways * step, axis=dim)
+        if 2 * far < ways:
+            going_down = lax.ppermute(going_down, axis, [(d, (d - 1) % ways) for d in range(ways)])
+            full = lax.dynamic_update_slice_in_dim(
+                full, going_down, (here + far) % ways * step, axis=dim
+            )
+    return full
 
 
 def normalize(residual, gain, shift):
@@ -179,7 +197,7 @@
         branch = lax.psum_scatter(attn_part + ffn_part, "tensor", scatter_dimension=0, tiled=True)
         output_rows = (residual + branch + dense_shift + fc2_shift).astype(jnp.bfloat16)
         back_set = current_set()
-        grad_full = lax.all_gather(rows_grad, "tensor", axis=0, tiled=True)
+        grad_full = gather_around(rows_grad, "tensor", 0)
         grad_dense = jnp.einsum("lhe,ld->hed", mixed, grad_full, preferred_element_type=jnp.float32)
         grad_mixed = jnp.einsum(
             "ld,hed->lhe", grad_full, back_set[2], preferred_element_type=jnp.float32

time: 2310 us -> 2220 us (0.961)
  waiting for transfers between devices: 1340 us -> 1200 us
  starting transfers between devices: 18.6 us -> 51.4 us
    all_gather x2 -> x0, waiting for transfers between devices: 165 us -> none  [micro_step(): grad_full = lax.all_gather(rows_grad, 'tensor', axis=0, tiled=True)]
    ppermute x0 -> x6, waiting for transfers between devices: none -> 142 us  [the longest x2 88.1 us: gather_around(): lax.ppermute(going_down, axis, [(d, (d - 1) % ways) for d in range(ways)])]
    all_gather x2, waiting for transfers between devices: 149 us -> 47.3 us  [micro_step(): lax.all_gather(normed_one.astype(jnp.bfloat16), 'tensor', axis=0, tiled=T...]
    ppermute x0 -> x6, starting transfers between devices: none -> 32.9 us  [the longest x4 26.8 us: gather_around(): lax.ppermute(going_up, axis, [(d, (d + 1) % ways) for d in range(ways)])]
  transfers between devices with their start and end apart: 30 -> 34, of which waited for: 19 -> 21; matrix products, arithmetic and copies ran while one was open for 30% -> 32% of each run, Pallas kernels for 0% -> 0%
where the time goes in v1:
time: 2220 us; the launch traced here: 2210 us
  waiting for transfers between devices  1200 us (54%)
  matrix products  387 us (17%)
  local copies, waits for them, and re-layouts  256 us (12%)
  blocking collectives  159 us (7%)
  other arithmetic  110 us (5%)
  starting transfers between devices  51.4 us (2%)
  loops' own time  25.3 us (1%)
    reduce_scatter x2, waiting for transfers between devices, micro_step(): lax.psum_scatter(grad_second, 'tensor', scatter_dimension=0, tiled=True)  295 us
    reduce_scatter x2, waiting for transfers between devices, micro_step(): lax.psum_scatter(attn_part + ffn_part, 'tensor', scatter_dimension=0, til...  287 us
    unnamed x2, blocking collectives  123 us
    all_gather x2, waiting for transfers between devices, current_set(): lax.all_gather(shard_set[0], 'dp', axis=0, tiled=True)  96.6 us
    dynamic_update_slice x8, local copies, waits for them, and re-layouts, micro_step(): lax.scan(back_block, (zero_heads, zero_heads), (starts, lse_blocks))  92.9 us
    ppermute x2, waiting for transfers between devices, gather_around(): lax.ppermute(going_down, axis, [(d, (d - 1) % ways) for d in range(ways)])  88.1 us
    reduce_scatter x2, waiting for transfers between devices, micro_step(): lax.psum_scatter(grad_first, 'tensor', scatter_dimension=0, tiled=True)  79.6 us
    reduce_scatter x1, waiting for transfers between devices, per_device(): lax.psum_scatter(weight_totals[5].astype(jnp.bfloat16), 'dp', scatter_dim...  72.2 us
  transfers between devices with their start and end apart: 34, of which 21 were waited for; matrix products, arithmetic and copies ran while one was open for 32% of the time, Pallas kernels for 0%

profile of v1, /device:TPU:0, one launch (start us, length us, event | category | flops | bytes accessed | tf_op | source)
XLA Modules:
  0.0 2209.2 jit_solution(6585401585072268613)
XLA Ops:
  28.8 23.3 %all-to-all-done = bf16[2,8,32,2048]{3,2,0,1:T(8,128)(2,1)S(1)} async-done(((bf16[2,8,32,2048]{3,2,0,1:T(8,128)(2,1)}), bf16[2,8,32,2048]{3,2,0,1:T(8,128)(2,1)S(1)}, u32[]{:S(2)}, u32[]{:S(2)}) %all-to-all-start) | async-done | bytes 2097184 | tf_op jit(solution)/shard_map/all_to_all | solution.py:106
  58.2 58.6 %all-reduce.14 = (bf16[2048]{0:T(1024)(128)(2,1)S(1)}, bf16[2048]{0:T(1024)(128)(2,1)S(1)}, bf16[2048]{0:T(1024)(128)(2,1)S(1)}, bf16[2048]{0:T(1024)(128)(2,1)S...) all-reduce(bf16[2048]{0:T(1024)(128)(2,1)S(1)} %dynamic-update-slic, ...), channel_id=1, replica_groups=mesh['dp'=8,'tensor'=4] {'dp','tensor'}, use_global_device_ids=true, to_apply=%add | all-reduce | flops 12288 | bytes 49152
  127.9 1681.2 %while.108 = (s32[]{:T(128)}, f32[2048,2,768]{2,0,1:T(8,128)}, f32[2,768]{1,0:T(2,128)}, f32[2,256,2048]{2,1,0:T(8,128)}, f32[2048,2048]{1,0:T(8,128)}, /*index=...) while((s32[]{:T(128)}, f32[2048,2,768]{2,0,1:T(8,128)}, ...), condition=%wide.region_24.26_spmd.clone.clone.clone.clone, body=%wide.region_0.25_spmd.clone.clone.clone.clone.sunk | while | flops 81338195968 | bytes 873498304 | solution.py:298
  170.9 58.8 %collective-permute-done.1 = bf16[256,2048]{1,0:T(8,128)(2,1)} collective-permute-done((bf16[256,2048]{1,0:T(8,128)(2,1)S(1)}, bf16[256,2048]{1,0:T(8,128)(2,1)}, u32[]{:S(2)}, u32[]{:S(2)}) %collective-permute-start.1) | collective-permute-done | bytes 1048608 | tf_op jit(solution)/shard_map/while/body/eval_jaxpr/ppermute | solution.py:27
  251.9 22.1 all-gather.15.cloned.1.call-done
  274.0 48.3 %all-gather.13.cloned.1.call-done = bf16[2048,2,768]{0,2,1:T(8,128)(2,1)} async-done(((bf16[256,2,768]{0,2,1:T(8,128)(2,1)}), bf16[2048,2,768]{0,2,1:T(8,128)(2,1)}) %all-gather.13.cloned.1.call-update) | async-done | bytes 6291472 | tf_op jit(solution)/shard_map/while/body/eval_jaxpr/all_gather | solution.py:124
  359.6 87.4 %while.110 = (s32[]{:T(128)}, f32[1024,2,256]{0,2,1:T(8,128)}, f32[1024,2,256]{0,2,1:T(8,128)}, f32[2,512,2,256]{1,0,3,2:T(2,128)}, s32[2]{0:T(128)S(1)}, /*inde...) while((s32[]{:T(128)}, f32[1024,2,256]{0,2,1:T(8,128)}, ...), condition=%wide.region_9.10_spmd.clone.clone, body=%wide.region_7.9_spmd.clone.clone.sunk | while | flops 2704015360 | bytes 111194568 | solution.py:259
  375.9 19.6 dynamic_update_slice.100
  418.3 19.6 dynamic_update_slice.100
  492.7 31.3 %fusion.251 = (bf16[1024,2048]{1,0:T(8,128)(2,1)}, f32[1024,2048]{1,0:T(8,128)}) fusion(f32[2048]{0:T(1024)S(1)} %bitcast.324, bf16[1024,2048]{1,0:T(8,128)(2,1)} %all-gather.19.cloned.1.call-done, bf16[2048,2048]{1,0:T(8,128)(2,1)} %all-gather.21.cloned.1.call-done), kind=kOutput, calls=%fused_computation.67.clone.1 | convolution fusion | flops 8728346624 | bytes 25174016 | tf_op jit(solution)/shard_map/while/body/eval_jaxpr/dot_general | solution.py:192
  619.4 44.9 %reduce-scatter.25.cloned.1.call-done = f32[256,2048]{1,0:T(8,128)} async-done(((f32[1024,2048]{1,0:T(8,128)}), f32[256,2048]{1,0:T(8,128)}) %reduce-scatter.25.cloned.1.call-update) | async-done | bytes 2097168 | tf_op jit(solution)/shard_map/while/body/eval_jaxpr/reduce_scatter | solution.py:277
  664.3 147.6 %reduce-scatter.23.cloned.1.call-done = f32[256,2048]{1,0:T(8,128)} async-done(((f32[1024,2048]{1,0:T(8,128)}), f32[256,2048]{1,0:T(8,128)}) %reduce-scatter.23.cloned.1.call-update) | async-done | bytes 2097168 | tf_op jit(solution)/shard_map/while/body/eval_jaxpr/reduce_scatter | solution.py:278
  816.1 143.4 %reduce-scatter.27.cloned.1.call-done = f32[256,2048]{1,0:T(8,128)} async-done(((f32[1024,2048]{1,0:T(8,128)}), f32[256,2048]{1,0:T(8,128)}) %reduce-scatter.27.cloned.1.call-update) | async-done | bytes 2097168 | tf_op jit(solution)/shard_map/while/body/eval_jaxpr/reduce_scatter | solution.py:197
  1001.0 24.7 %collective-permute-start.2 = (bf16[256,2048]{1,0:T(8,128)(2,1)S(1)}, bf16[256,2048]{1,0:T(8,128)(2,1)S(1)}, u32[]{:S(2)}, u32[]{:S(2)}) collective-permute-start(bf16[256,2048]{1,0:T(8,128)(2,1)S(1)} %collective-permute-done), channel_id=1, source_target_pairs={{0,1},{1,2},{2,3},{3,0},{4,5},{5,6},{6,7},{7,4},{8,9},{9,10},{10,1... | collective-permute-start | bytes 3145736 | tf_op jit(solution)/shard_map/while/body/eval_jaxpr/ppermute | solution.py:24
  1031.5 29.3 %collective-permute-done.1 = bf16[256,2048]{1,0:T(8,128)(2,1)} collective-permute-done((bf16[256,2048]{1,0:T(8,128)(2,1)S(1)}, bf16[256,2048]{1,0:T(8,128)(2,1)}, u32[]{:S(2)}, u32[]{:S(2)}) %collective-permute-start.1) | collective-permute-done | bytes 1048608 | tf_op jit(solution)/shard_map/while/body/eval_jaxpr/ppermute | solution.py:27
  1087.4 25.2 %all-gather.15.cloned.1.call-done = bf16[1024,2048]{1,0:T(8,128)(2,1)} async-done(((bf16[256,2048]{1,0:T(8,128)(2,1)}), bf16[1024,2048]{1,0:T(8,128)(2,1)}) %all-gather.15.cloned.1.call-update) | async-done | bytes 4194320 | tf_op jit(solution)/shard_map/while/body/eval_jaxpr/all_gather | solution.py:159
  1112.6 48.3 %all-gather.13.cloned.1.call-done = bf16[2048,2,768]{0,2,1:T(8,128)(2,1)} async-done(((bf16[256,2,768]{0,2,1:T(8,128)(2,1)}), bf16[2048,2,768]{0,2,1:T(8,128)(2,1)}) %all-gather.13.cloned.1.call-update) | async-done | bytes 6291472 | tf_op jit(solution)/shard_map/while/body/eval_jaxpr/all_gather | solution.py:124
  1179.8 17.4 while.109
  1198.2 87.4 %while.110 = (s32[]{:T(128)}, f32[1024,2,256]{0,2,1:T(8,128)}, f32[1024,2,256]{0,2,1:T(8,128)}, f32[2,512,2,256]{1,0,3,2:T(2,128)}, s32[2]{0:T(128)S(1)}, /*inde...) while((s32[]{:T(128)}, f32[1024,2,256]{0,2,1:T(8,128)}, ...), condition=%wide.region_9.10_spmd.clone.clone, body=%wide.region_7.9_spmd.clone.clone.sunk | while | flops 2704015360 | bytes 111194568 | solution.py:259
  1214.6 19.6 dynamic_update_slice.100
  1257.0 19.7 dynamic_update_slice.100
  1331.4 31.4 %fusion.251 = (bf16[1024,2048]{1,0:T(8,128)(2,1)}, f32[1024,2048]{1,0:T(8,128)}) fusion(f32[2048]{0:T(1024)S(1)} %bitcast.324, bf16[1024,2048]{1,0:T(8,128)(2,1)} %all-gather.19.cloned.1.call-done, bf16[2048,2048]{1,0:T(8,128)(2,1)} %all-gather.21.cloned.1.call-done), kind=kOutput, calls=%fused_computation.67.clone.1 | convolution fusion | flops 8728346624 | bytes 25174016 | tf_op jit(solution)/shard_map/while/body/eval_jaxpr/dot_general | solution.py:192
  1433.8 18.4 select_add_fusion.26
  1468.3 34.6 %reduce-scatter.25.cloned.1.call-done = f32[256,2048]{1,0:T(8,128)} async-done(((f32[1024,2048]{1,0:T(8,128)}), f32[256,2048]{1,0:T(8,128)}) %reduce-scatter.25.cloned.1.call-update) | async-done | bytes 2097168 | tf_op jit(solution)/shard_map/while/body/eval_jaxpr/reduce_scatter | solution.py:277
  1503.0 147.4 %reduce-scatter.23.cloned.1.call-done = f32[256,2048]{1,0:T(8,128)} async-done(((f32[1024,2048]{1,0:T(8,128)}), f32[256,2048]{1,0:T(8,128)}) %reduce-scatter.23.cloned.1.call-update) | async-done | bytes 2097168 | tf_op jit(solution)/shard_map/while/body/eval_jaxpr/reduce_scatter | solution.py:278
  1654.6 143.2 %reduce-scatter.27.cloned.1.call-done = f32[256,2048]{1,0:T(8,128)} async-done(((f32[1024,2048]{1,0:T(8,128)}), f32[256,2048]{1,0:T(8,128)}) %reduce-scatter.27.cloned.1.call-update) | async-done | bytes 2097168 | tf_op jit(solution)/shard_map/while/body/eval_jaxpr/reduce_scatter | solution.py:197
  1816.4 21.9 copy.230
  1870.6 22.5 %all-to-all-done.3 = bf16[2,1,256,2048]{3,0,1,2:T(2,128)(2,1)S(1)} async-done(((bf16[2,1,256,2048]{3,0,1,2:T(2,128)(2,1)}), bf16[2,1,256,2048]{3,0,1,2:T(2,128)(2,1)S(1)}, u32[]{:S(2)}, u32[]{:S(2)}) %all-to-all-start.3) | async-done | bytes 2097184 | tf_op jit(solution)/shard_map/all_to_all | solution.py:324
  1899.0 64.1 %all-reduce.13 = (f32[2048]{0:T(1024)S(1)}, f32[2048]{0:T(1024)S(1)}, f32[2048]{0:T(1024)S(1)}, f32[2048]{0:T(1024)S(1)}, f32[2048]{0:T(1024)S(1)}, /*index=5*/f32[2048]{0:T(1024)S(1)}) all-reduce(f32[2048]{0:T(1024)S(1)} %copy-done.34, f32[2048]{0:T(1024)S(1)} %copy-done.37, ...), channel_id=5, replica_groups=mesh['dp'=8,'tensor'=4] {'dp','tensor'}, use_global_device_ids=true, to_apply=%region_26.28.clone | all-reduce | flops 12288 | bytes 98304
  1986.4 62.7 %all-reduce.17.cloned.1.call-done = bf16[2048,2,768]{2,1,0:T(2,128)(2,1)} async-done(((bf16[2048,2,768]{2,1,0:T(2,128)(2,1)}), bf16[2048,2,768]{2,1,0:T(2,128)(2,1)}) %all-reduce.17.cloned.1.call-update) | async-done | bytes 6291472
  2051.9 72.0 %reduce-scatter.15.cloned.1.call-done = bf16[256,2048]{1,0:T(8,128)(2,1)} async-done(((bf16[2048,2048]{1,0:T(8,128)(2,1)}), bf16[256,2048]{1,0:T(8,128)(2,1)}) %reduce-scatter.15.cloned.1.call-update) | async-done | bytes 1048592 | tf_op jit(solution)/shard_map/reduce_scatter | solution.py:311
  2126.6 72.2 %reduce-scatter.17.cloned.1.call-done = bf16[2048,256]{1,0:T(8,128)(2,1)} async-done(((bf16[2048,2048]{1,0:T(8,128)(2,1)}), bf16[2048,256]{1,0:T(8,128)(2,1)}) %reduce-scatter.17.cloned.1.call-update) | async-done | bytes 1048592 | tf_op jit(solution)/shard_map/reduce_scatter | solution.py:317
  (645 shorter events, 709.6 us)
Async XLA Ops:
  20.3 31.8 %all-to-all-start = ((bf16[2,8,32,2048]{3,2,0,1:T(8,128)(2,1)}), bf16[2,8,32,2048]{3,2,0,1:T(8,128)(2,1)S(1)}, u32[]{:S(2)}, u32[]{:S(2)}) async-start(bf16[2,8,32,2048]{3,2,0,1:T(8,128)(2,1)} %copy.186), calls=%async_computation.3 | async-start | bytes 4194304 | tf_op jit(solution)/shard_map/all_to_all | solution.py:106
  52.1 72.6 %all-to-all-start.1 = ((bf16[2,8,32,2048]{3,2,0,1:T(8,128)(2,1)}), bf16[2,8,32,2048]{3,2,0,1:T(8,128)(2,1)}, u32[]{:S(2)}, u32[]{:S(2)}) async-start(bf16[2,8,32,2048]{3,2,0,1:T(8,128)(2,1)} %copy.188), calls=%async_computation.4 | async-start | bytes 4194304 | tf_op jit(solution)/shard_map/all_to_all | solution.py:107
  128.3 117.4 %all-gather.17.cloned.1.call-start = ((), (), s32[]{:S(2)}) async-start(), calls=%async_computation.20 | async-start | bytes 2359296 | tf_op jit(solution)/shard_map/while/body/eval_jaxpr/all_gather | solution.py:126
  129.0 145.0 %all-gather.15.cloned.1.call-start = ((), (), s32[]{:S(2)}) async-start(), calls=%async_computation.19 | async-start | bytes 5242880 | tf_op jit(solution)/shard_map/while/body/eval_jaxpr/all_gather | solution.py:159
  132.7 189.6 %all-gather.13.cloned.1.call-start = ((), (), s32[]{:S(2)}) async-start(), calls=%async_computation.18 | async-start | bytes 7077888 | tf_op jit(solution)/shard_map/while/body/eval_jaxpr/all_gather | solution.py:124
  133.4 359.3 %all-gather.19.cloned.1.call-start = ((), (), s32[]{:S(2)}) async-start(), calls=%async_computation.21 | async-start | bytes 5242880 | tf_op jit(solution)/shard_map/while/body/eval_jaxpr/all_gather | solution.py:160
  134.0 358.7 %all-gather.21.cloned.1.call-start = ((), (), s32[]{:S(2)}) async-start(), calls=%async_computation.22 | async-start | bytes 9437184 | tf_op jit(solution)/shard_map/while/body/eval_jaxpr/all_gather | solution.py:127
  134.6 389.5 %all-gather.23.cloned.1.call-start = ((), (), s32[]{:S(2)}) async-start(), calls=%async_computation.23 | async-start | bytes 9437184 | tf_op jit(solution)/shard_map/while/body/eval_jaxpr/all_gather | solution.py:129
  137.1 92.7 %collective-permute-start.1 = (bf16[256,2048]{1,0:T(8,128)(2,1)S(1)}, bf16[256,2048]{1,0:T(8,128)(2,1)}, u32[]{:S(2)}, u32[]{:S(2)}) collective-permute-start(bf16[256,2048]{1,0:T(8,128)(2,1)S(1)} %get-tuple-element.2041), channel_id=1, source_target_pairs={{0,3},{1,0},{2,1},{3,2},{4,7},{5,4},{6,5},{7,6},{8,11},{9,8},{10,9... | collective-permute-start | bytes 3145736 | tf_op jit(solution)/shard_map/while/body/eval_jaxpr/ppermute | solution.py:27
  140.5 523.8 %reduce-scatter.25.cloned.1.call-start = ((), (), s32[]{:S(2)}) async-start(), calls=%async_computation.25 | async-start | bytes 10485760 | tf_op jit(solution)/shard_map/while/body/eval_jaxpr/reduce_scatter | solution.py:277
  164.5 80.1 %collective-permute-start.2 = (bf16[256,2048]{1,0:T(8,128)(2,1)S(1)}, bf16[256,2048]{1,0:T(8,128)(2,1)S(1)}, u32[]{:S(2)}, u32[]{:S(2)}) collective-permute-start(bf16[256,2048]{1,0:T(8,128)(2,1)S(1)} %collective-permute-done), channel_id=1, source_target_pairs={{0,1},{1,2},{2,3},{3,0},{4,5},{5,6},{6,7},{7,4},{8,9},{9,10},{10,1... | collective-permute-start | bytes 3145736 | tf_op jit(solution)/shard_map/while/body/eval_jaxpr/ppermute | solution.py:24
  483.3 328.7 %reduce-scatter.23.cloned.1.call-start = ((), (), s32[]{:S(2)}) async-start(), calls=%async_computation.24 | async-start | bytes 10485760 | tf_op jit(solution)/shard_map/while/body/eval_jaxpr/reduce_scatter | solution.py:278
  554.4 405.1 %reduce-scatter.27.cloned.1.call-start = ((), (), s32[]{:S(2)}) async-start(), calls=%async_computation.26 | async-start | bytes 10485760 | tf_op jit(solution)/shard_map/while/body/eval_jaxpr/reduce_scatter | solution.py:197
  964.9 116.2 %all-gather.17.cloned.1.call-start = ((), (), s32[]{:S(2)}) async-start(), calls=%async_computation.20 | async-start | bytes 2359296 | tf_op jit(solution)/shard_map/while/body/eval_jaxpr/all_gather | solution.py:126
  965.5 147.1 %all-gather.15.cloned.1.call-start = ((), (), s32[]{:S(2)}) async-start(), calls=%async_computation.19 | async-start | bytes 5242880 | tf_op jit(solution)/shard_map/while/body/eval_jaxpr/all_gather | solution.py:159
  969.1 191.8 %all-gather.13.cloned.1.call-start = ((), (), s32[]{:S(2)}) async-start(), calls=%async_computation.18 | async-start | bytes 7077888 | tf_op jit(solution)/shard_map/while/body/eval_jaxpr/all_gather | solution.py:124
  969.7 361.7 %all-gather.19.cloned.1.call-start = ((), (), s32[]{:S(2)}) async-start(), calls=%async_computation.21 | async-start | bytes 5242880 | tf_op jit(solution)/shard_map/while/body/eval_jaxpr/all_gather | solution.py:160
  970.5 360.9 %all-gather.21.cloned.1.call-start = ((), (), s32[]{:S(2)}) async-start(), calls=%async_computation.22 | async-start | bytes 9437184 | tf_op jit(solution)/shard_map/while/body/eval_jaxpr/all_gather | solution.py:127
  971.0 391.8 %all-gather.23.cloned.1.call-start = ((), (), s32[]{:S(2)}) async-start(), calls=%async_computation.23 | async-start | bytes 9437184 | tf_op jit(solution)/shard_map/while/body/eval_jaxpr/all_gather | solution.py:129
  974.3 86.5 %collective-permute-start.1 = (bf16[256,2048]{1,0:T(8,128)(2,1)S(1)}, bf16[256,2048]{1,0:T(8,128)(2,1)}, u32[]{:S(2)}, u32[]{:S(2)}) collective-permute-start(bf16[256,2048]{1,0:T(8,128)(2,1)S(1)} %get-tuple-element.2041), channel_id=1, source_target_pairs={{0,3},{1,0},{2,1},{3,2},{4,7},{5,4},{6,5},{7,6},{8,11},{9,8},{10,9... | collective-permute-start | bytes 3145736 | tf_op jit(solution)/shard_map/while/body/eval_jaxpr/ppermute | solution.py:27
  977.0 526.0 %reduce-scatter.25.cloned.1.call-start = ((), (), s32[]{:S(2)}) async-start(), calls=%async_computation.25 | async-start | bytes 10485760 | tf_op jit(solution)/shard_map/while/body/eval_jaxpr/reduce_scatter | solution.py:277
  1001.0 79.0 %collective-permute-start.2 = (bf16[256,2048]{1,0:T(8,128)(2,1)S(1)}, bf16[256,2048]{1,0:T(8,128)(2,1)S(1)}, u32[]{:S(2)}, u32[]{:S(2)}) collective-permute-start(bf16[256,2048]{1,0:T(8,128)(2,1)S(1)} %collective-permute-done), channel_id=1, source_target_pairs={{0,1},{1,2},{2,3},{3,0},{4,5},{5,6},{6,7},{7,4},{8,9},{9,10},{10,1... | collective-permute-start | bytes 3145736 | tf_op jit(solution)/shard_map/while/body/eval_jaxpr/ppermute | solution.py:24
  1322.0 328.4 %reduce-scatter.23.cloned.1.call-start = ((), (), s32[]{:S(2)}) async-start(), calls=%async_computation.24 | async-start | bytes 10485760 | tf_op jit(solution)/shard_map/while/body/eval_jaxpr/reduce_scatter | solution.py:278
  1393.2 404.6 %reduce-scatter.27.cloned.1.call-start = ((), (), s32[]{:S(2)}) async-start(), calls=%async_computation.26 | async-start | bytes 10485760 | tf_op jit(solution)/shard_map/while/body/eval_jaxpr/reduce_scatter | solution.py:197
  1809.1 157.4 %reduce-scatter.19.cloned.1.call-start = ((), (), s32[]{:S(2)}) async-start(), calls=%async_computation.15 | async-start | bytes 221184
  1810.8 157.2 %reduce-scatter.21.cloned.1.call-start = ((), (), s32[]{:S(2)}) async-start(), calls=%async_computation.16 | async-start | bytes 294912
  1812.4 171.9 %reduce-scatter.13.cloned.1.call-start = ((), (), s32[]{:S(2)}) async-start(), calls=%async_computation.12 | async-start | bytes 2359296 | tf_op jit(solution)/shard_map/reduce_scatter | solution.py:308
  1816.3 232.7 %all-reduce.17.cloned.1.call-start = ((), (), s32[]{:S(2)}) async-start(), calls=%async_computation.17 | async-start | bytes 12582912
  1838.3 285.5 %reduce-scatter.15.cloned.1.call-start = ((), (), s32[]{:S(2)}) async-start(), calls=%async_computation.13 | async-start | bytes 9437184 | tf_op jit(solution)/shard_map/reduce_scatter | solution.py:311
  1847.5 351.4 %reduce-scatter.17.cloned.1.call-start = ((), (), s32[]{:S(2)}) async-start(), calls=%async_computation.14 | async-start | bytes 9437184 | tf_op jit(solution)/shard_map/reduce_scatter | solution.py:317
  1861.7 31.4 %all-to-all-start.3 = ((bf16[2,1,256,2048]{3,0,1,2:T(2,128)(2,1)}), bf16[2,1,256,2048]{3,0,1,2:T(2,128)(2,1)S(1)}, u32[]{:S(2)}, u32[]{:S(2)}) async-start(bf16[2,1,256,2048]{3,0,1,2:T(2,128)(2,1)} %bitcast.315), calls=%async_computation.6 | async-start | bytes 4194304 | tf_op jit(solution)/shard_map/all_to_all | solution.py:324
  1893.1 82.0 %all-to-all-start.2 = ((bf16[2,1,256,2048]{3,0,1,2:T(2,128)(2,1)}), bf16[2,1,256,2048]{3,0,1,2:T(2,128)(2,1)}, u32[]{:S(2)}, u32[]{:S(2)}) async-start(bf16[2,1,256,2048]{3,0,1,2:T(2,128)(2,1)} %bitcast.314), calls=%async_computation.5 | async-start | bytes 4194304 | tf_op jit(solution)/shard_map/all_to_all | solution.py:323
  (139 other events, 7749.0 us)
Sparse Core Ops, SparseCore 0:
  131.0 26.9 all-gather.16
  159.6 114.3 all-gather.14
  275.8 46.3 all-gather.12
  324.2 80.7 all-gather.18
  406.8 52.9 all-gather.20
  461.5 55.9 all-gather.22
  519.8 144.4 reduce-scatter.24
  666.7 145.2 reduce-scatter.22
  814.3 145.1 reduce-scatter.26
  967.3 28.6 all-gather.16
  997.5 115.0 all-gather.14
  1114.3 46.5 all-gather.12
  1163.0 80.7 all-gather.18
  1245.6 52.9 all-gather.20
  1300.2 55.9 all-gather.22
  1358.4 144.4 reduce-scatter.24
  1505.2 145.1 reduce-scatter.22
  1652.6 145.1 reduce-scatter.26
Sparse Core Ops, SparseCore 1:
  1813.2 34.2 reduce-scatter.18
  1851.3 34.6 reduce-scatter.20
  1889.1 51.9 reduce-scatter.12
  1944.7 104.3 all-reduce.16
  2052.6 71.2 reduce-scatter.14
  2127.7 71.1 reduce-scatter.16
